TPU v7x, 32 devices: a whole 2x2x4 slice. The times are simulated.
32 devices in a mesh: groups: 2 (over y), lon: 4 (over z), lat: 2 (over x), dp: 2 (over core).
Axes of the slice: x: 2, y: 2, z: 4, core: 2. Of those that a mesh axis runs over, the one named last changes fastest.
Arguments:
- inputs: bfloat16 [4, 128, 1024, 128], P(('groups', 'dp'), 'lat', 'lon'), parts along dimension 0, may hold values from -6 to 6
- cotangent: bfloat16 [4, 128, 1024, 128], P(('groups', 'dp'), 'lat', 'lon'), parts along dimension 0, may hold values from -6 to 6
- kernel_dw: bfloat16 [7, 7, 128], replicated, may hold values from -0.875 to 0.875
- bias_dw: float32 [128], replicated, may hold values from -3 to 3
- gain: float32 [128], replicated, may hold values from 0.1 to 1.9
- shift_ln: float32 [128], replicated, may hold values from -2 to 2
- w_in: bfloat16 [128, 256], replicated, may hold values from -0.5 to 0.5
- b_in: float32 [256], replicated, may hold values from -2 to 2
- w_out: bfloat16 [256, 128], replicated, may hold values from -0.375 to 0.375
- ocean_mask: int32 [2, 16], P('lat', 'lon'), may hold values from 0 to 1, as said below
Outputs:
- grad_inputs: bfloat16 [4, 128, 1024, 128], P(('groups', 'dp'), 'lat', 'lon'), parts along dimension 0
- grad_w_in: float32 [256, 256], P(('groups', 'dp')), parts along dimension 0
- grad_w_out: float32 [512, 128], P(('groups', 'dp')), parts along dimension 0
- grad_kernel: float32 [14, 7, 128], P('groups'), parts along dimension 0
- grad_bias_dw: float32 [256], P('groups'), parts along dimension 0
- grad_gain: float32 [256], P('groups'), parts along dimension 0
- grad_shift: float32 [256], P('groups'), parts along dimension 0
- grad_b_in: float32 [512], P('groups'), parts along dimension 0
There are 2 independent parts, one for each index of `groups`. A program takes and returns all parts, laid end to end along the dimension named above; an argument that names none is the same for every part. Nothing has to cross between parts.
Inputs may be any that keep to these rules, and one draw needn't show every extreme that they name: `ocean_mask`: every block of the northernmost block row (index 1) is ocean, and each aligned run of 4 blocks of a block row holds at least one ocean block.
All inputs are finite; a program needn't handle non-finite values.
Results may differ from a plain program's by a relative error of at most 0.0056.
Values may be sent and summed in bfloat16 or wider, within the bound.
A program may use at most 128 MiB of HBM per device.

v0:
```python
import math
import jax
import jax.numpy as jnp
from jax import lax
from jax.sharding import PartitionSpec as P

KS = 7
EPS = 1e-06
GELU_K = 0.7978845608
GELU_C = 0.044715


def padded(block, sides, width, periodic):
    for axis, dim in sides:
        count = lax.axis_size(axis)
        forward = [(i, i + 1) for i in range(count - 1)]
        if periodic:
            forward.append((count - 1, 0))
        backward = [(target, source) for source, target in forward]
        low = lax.ppermute(
            lax.slice_in_dim(block, block.shape[dim] - width, None, axis=dim), axis, forward
        )
        high = lax.ppermute(lax.slice_in_dim(block, 0, width, axis=dim), axis, backward)
        block = jnp.concatenate([low, block, high], axis=dim)
    return block


def partner(block, axis, stride):
    count = lax.axis_size(axis)
    route = []
    for low in range(count):
        high = low | 1 << stride
        if high != low and high < count:
            route += [(low, high), (high, low)]
    return lax.ppermute(block, axis, route)


def extend(field):
    half = KS // 2
    rows = field.shape[1]
    framed = padded(field, (("lat", 1),), half, False)
    mirror = field[:, rows - half :]
    for bit in range(lax.axis_size("lon").bit_length() - 1):
        mirror = partner(mirror, "lon", bit)
    band = mirror[:, ::-1, ::-1, :]
    northern = lax.axis_index("lat") == lax.axis_size("lat") - 1
    upper = jnp.where(northern, band, framed[:, rows + half :])
    framed = jnp.concatenate([framed[:, : rows + half], upper], 1)
    return padded(framed, (("lon", 2),), half, True)


def conv_valid(extended, kernel):
    return lax.conv_general_dilated(
        extended,
        kernel[:, :, None, :],
        (1, 1),
        "VALID",
        dimension_numbers=("NHWC", "HWIO", "NHWC"),
        feature_group_count=extended.shape[3],
        preferred_element_type=jnp.float32,
    )


def kernel_grad(extended, delta):
    out = lax.conv_general_dilated(
        extended[None],
        delta[:, :, None, :],
        (1, 1),
        "VALID",
        dimension_numbers=("NHWC", "HWIO", "NHWC"),
        feature_group_count=extended.shape[2],
        preferred_element_type=jnp.float32,
    )
    return out[0]


def cell_grads(ycells, gcells, maskval, gain, shift_ln, w_in, b_in, w_out):
    center = ycells - jnp.mean(ycells, -1, keepdims=True)
    rstd = lax.rsqrt(jnp.mean(center * center, -1, keepdims=True) + EPS)
    nhat = center * rstd
    normed = (nhat * gain + shift_ln).astype(jnp.bfloat16)
    pre = jnp.dot(normed, w_in, preferred_element_type=jnp.float32) + b_in
    tangent = jnp.tanh(GELU_K * (pre + GELU_C * pre * pre * pre))
    act = (0.5 * pre * (1.0 + tangent)).astype(jnp.bfloat16)
    outgrad = (gcells.astype(jnp.float32) * maskval).astype(jnp.bfloat16)
    g_out = lax.dot_general(
        act, outgrad, (((0,), (0,)), ((), ())), preferred_element_type=jnp.float32
    )
    dact = lax.dot_general(
        outgrad, w_out, (((1,), (1,)), ((), ())), preferred_element_type=jnp.float32
    )
    slope = 0.5 * (1.0 + tangent) + 0.5 * pre * (1.0 - tangent * tangent) * GELU_K * (
        1.0 + 3.0 * GELU_C * pre * pre
    )
    dpre = dact * slope
    dpre_b = dpre.astype(jnp.bfloat16)
    g_in = lax.dot_general(
        normed, dpre_b, (((0,), (0,)), ((), ())), preferred_element_type=jnp.float32
    )
    g_bin = jnp.sum(dpre, 0)
    dnorm = lax.dot_general(
        dpre_b, w_in, (((1,), (1,)), ((), ())), preferred_element_type=jnp.float32
    )
    g_gain = jnp.sum(dnorm * nhat, 0)
    g_shift = jnp.sum(dnorm, 0)
    dscaled = dnorm * gain
    delta = rstd * (
        dscaled
        - jnp.mean(dscaled, -1, keepdims=True)
        - nhat * jnp.mean(dscaled * nhat, -1, keepdims=True)
    )
    return (delta.astype(jnp.bfloat16), (g_in, g_bin, g_out, g_gain, g_shift))


def local(inputs, cotangent, kernel_dw, bias_dw, gain, shift_ln, w_in, b_in, w_out, ocean_mask):
    batch, rows, cols, chans = inputs.shape
    hidden = w_in.shape[1]
    half = KS // 2
    per_tile = cols // rows
    extended = extend(inputs)
    field_y = conv_valid(extended, kernel_dw) + bias_dw

    def to_blocks(field):
        parts = field.reshape(batch, rows, per_tile, rows, chans).transpose(0, 2, 1, 3, 4)
        return parts.reshape(batch * per_tile, rows * rows, chans)

    masks = jnp.tile(ocean_mask.reshape(-1), batch).astype(jnp.float32)
    totals = (
        jnp.zeros((chans, hidden), jnp.float32),
        jnp.zeros((hidden,), jnp.float32),
        jnp.zeros((hidden, chans), jnp.float32),
        jnp.zeros((chans,), jnp.float32),
        jnp.zeros((chans,), jnp.float32),
    )

    def step(carry, items):
        ycells, gcells, maskval = items
        delta, grads = cell_grads(ycells, gcells, maskval, gain, shift_ln, w_in, b_in, w_out)
        return (tuple((c + g for c, g in zip(carry, grads))), delta)

    totals, deltas = lax.scan(step, totals, (to_blocks(field_y), to_blocks(cotangent), masks))
    delta = (
        deltas.reshape(batch, per_tile, rows, rows, chans)
        .transpose(0, 2, 1, 3, 4)
        .reshape(batch, rows, cols, chans)
    )
    g_kernel = jnp.zeros((KS, KS, chans), jnp.float32)
    g_kernel = g_kernel + kernel_grad(extended[0], delta[0])
    g_bias = jnp.sum(delta.astype(jnp.float32), (0, 1, 2))
    spread = extend(delta)
    northern = lax.axis_index("lat") == lax.axis_size("lat") - 1
    fold_rows = spread[:, rows + half :]
    direct_part = jnp.concatenate(
        [spread[:, : rows + half], jnp.where(northern, jnp.zeros_like(fold_rows), fold_rows)], 1
    )
    direct = conv_valid(direct_part, kernel_dw[::-1, ::-1])
    fold_part = jnp.concatenate(
        [
            jnp.zeros_like(spread[:, rows - half : rows + half]),
            jnp.where(northern, fold_rows, jnp.zeros_like(fold_rows)),
        ],
        1,
    )
    fold = conv_valid(fold_part, kernel_dw)
    total = cotangent.astype(jnp.float32) + direct
    total = total.at[:, rows - half :].add(fold)
    grad_inputs = total.astype(jnp.bfloat16)
    g_in, g_bin, g_out, g_gain, g_shift = totals
    cells_all = (
        lax.axis_size("dp") * batch * lax.axis_size("lat") * rows * lax.axis_size("lon") * cols
    )
    scale = 1.0 / math.sqrt(cells_all)
    in_share = chans // lax.axis_size("dp")
    out_share = hidden // lax.axis_size("dp")
    summed = lax.psum((g_in, g_out, g_kernel, g_bias, g_gain, g_shift, g_bin), ("lon", "lat", "dp"))
    s_in, s_out, s_kernel, s_bias, s_gain, s_shift, s_bin = summed
    position = lax.axis_index("dp")
    s_in = lax.dynamic_slice_in_dim(s_in, position * in_share, in_share, 0)
    s_out = lax.dynamic_slice_in_dim(s_out, position * out_share, out_share, 0)
    return (
        grad_inputs,
        s_in * scale,
        s_out * scale,
        s_kernel * scale,
        s_bias * scale,
        s_gain * scale,
        s_shift * scale,
        s_bin * scale,
    )


def solution(mesh):
    placed = (
        P(("groups", "dp"), "lat", "lon", None),
        P(("groups", "dp"), "lat", "lon", None),
        P(),
        P(),
        P(),
        P(),
        P(),
        P(),
        P(),
        P("lat", "lon"),
    )
    return jax.shard_map(
        local,
        mesh=mesh,
        in_specs=placed,
        out_specs=(
            P(("groups", "dp"), "lat", "lon", None),
            P(("groups", "dp"), None),
            P(("groups", "dp"), None),
            P("groups", None, None),
            P("groups"),
            P("groups"),
            P("groups"),
            P("groups"),
        ),
        check_vma=False,
    )
```

profile of v0, /device:TPU:0, one launch (start us, length us, event | category | flops | bytes accessed | tf_op | source)
XLA Modules:
  0.0 606.1 jit_solution(1043596594227008258)
XLA Ops:
  7.2 7.8 %copy.54 = bf16[1,64,256,128]{3,0,2,1:T(2,128)(2,1)S(1)} copy(bf16[1,64,256,128]{3,2,1,0:T(8,128)(2,1)} %param.14) | data formatting | bytes 8388608 | tf_op args[0]
  23.4 7.8 %collective-permute-done.1 = bf16[1,3,256,128]{3,0,2,1:T(2,128)(2,1)S(1)} collective-permute-done((bf16[1,3,256,128]{3,0,2,1:T(2,128)(2,1)S(1)}, bf16[1,3,256,128]{3,0,2,1:T(2,128)(2,1)S(1)}, u32[]{:S(2)}, u32[]{:S(2)}) %collective-permute-start.1) | collective-permute-done | bytes 196640 | tf_op jit(solution)/shard_map/ppermute | solution.py:35
  37.4 13.4 %collective-permute-done.2 = bf16[1,3,256,128]{3,0,2,1:T(2,128)(2,1)S(1)} collective-permute-done((bf16[1,3,256,128]{3,0,2,1:T(2,128)(2,1)S(1)}, bf16[1,3,256,128]{3,0,2,1:T(2,128)(2,1)S(1)}, u32[]{:S(2)}, u32[]{:S(2)}) %collective-permute-start.2) | collective-permute-done | bytes 196640 | tf_op jit(solution)/shard_map/ppermute | solution.py:35
  57.4 5.5 copy.64
  62.9 41.8 %pad_maximum_fusion = bf16[1,70,262,128]{3,0,2,1:T(2,128)(2,1)S(1)} fusion(bf16[1,70,3,128]{3,0,2,1:T(2,128)(2,1)S(1)} %collective-permute-done.5, bf16[1,3,256,128]{3,0,2,1:T(2,128)(2,1)S(1)} %broadcast_select_fusion.4, bf16[1,64,256,128]{3,0,2,1:T(2,128)(2,1)} %copy-done, bf16[1,3,256,128]{3,0,2,1:T(2,128)(2,1)S(1)} %collective-permute-done, ...), kind=kLoop, calls=%fused_computation.47 | loop fusion | flops 9390080 | bytes 9390080 | tf_op jit(solution)/shard_map/concatenate | solution.py:24
  110.8 34.0 %select_add_fusion.1 = f32[64,8,33,128]{3,1,2,0:T(8,128)S(1)} fusion(f32[128]{0:T(128)S(1)} %copy-done.20, pred[8,33]{0,1:T(8,128)(4,1)S(1)} %copy-done.21, bf16[70,1,7,6,128]{4,2,3,0,1:T(8,128)(2,1)S(1)} %slice.80, bf16[70,1,8,33,128]{4,2,3,0,1:T(8,128)(2,1)S(1)} %copy.59, bf16[7,7,1,128]{3,1,0,2:T(8,128)(2,1)S(1)} %bitcast.144), kind=kOutput, calls=%fused_computation.48 | convolution fusion | flops 233041920 | bytes 14147592 | tf_op jit(solution)/shard_map/conv_general_dilated | solution.py:53
  148.2 4.9 copy.62
  153.1 4.2 copy.63
  157.3 98.5 %while.22 = (s32[]{:T(128)}, f32[128,256]{1,0:T(8,128)S(1)}, f32[256]{0:T(256)S(1)}, f32[256,128]{1,0:T(8,128)S(1)}, f32[128]{0:T(128)S(1)}, /*index=5*/f32[128]...) while((s32[]{:T(128)}, f32[128,256]{1,0:T(8,128)S(1)}, ...), condition=%wide.region_8.9_spmd.clone, body=%wide.region_0.8_spmd.clone.sunk | while | flops 1393168896 | bytes 81850672 | solution.py:141
  178.1 4.1 fusion.106
  202.6 4.1 fusion.106
  227.1 4.1 fusion.106
  251.6 4.1 fusion.106
  255.8 4.5 convert_reduce_fusion
  265.4 90.3 %fusion.29 = f32[1,7,7,128]{3,0,2,1:T(1,128)S(1)} fusion(bf16[1,70,262,128]{3,0,2,1:T(2,128)(2,1)} %copy-done.3, bf16[64,256,1,128]{3,1,0,2:T(8,128)(2,1)S(1)} %bitcast.128), kind=kOutput, calls=%fused_computation.51 | convolution fusion | flops 205520896 | bytes 8914432 | tf_op jit(solution)/shard_map/conv_general_dilated | solution.py:65
  355.8 57.7 %all-reduce = (f32[7,7,128]{2,1,0:T(8,128)S(1)}, f32[128]{0:T(128)S(1)}, f32[128]{0:T(128)S(1)}, f32[128]{0:T(128)S(1)}, f32[256]{0:T(256)S(1)}) all-reduce(f32[7,7,128]{2,1,0:T(8,128)S(1)} %bitcast.143, f32[128]{0:T(128)S(1)} %convert_reduce_fusion, ...), channel_id=1, replica_groups=mesh['groups'=2,'lon'=4,'lat'=2,'dp'=2] {'lon','lat','dp'}, use_global_device_ids=true, to_apply=%region_11.12 | all-reduce | flops 6912 | bytes 55296 | tf_op jit(solution)/shard_map/psum | solution.py:175
  417.3 91.0 %all-reduce.4.cloned.1.call-done = (f32[128,256]{1,0:T(8,128)}, f32[256,128]{1,0:T(8,128)}) async-done(((f32[128,256]{1,0:T(8,128)}, f32[256,128]{1,0:T(8,128)}), (f32[128,256]{1,0:T(8,128)}, f32[256,128]{1,0:T(8,128)})) %all-reduce.4.cloned.1.call-update) | async-done | bytes 262160 | tf_op jit(solution)/shard_map/psum | solution.py:175
  519.2 5.8 pad_maximum_fusion.1
  534.1 33.5 %broadcast_select_fusion.2 = f32[64,8,33,128]{3,1,2,0:T(8,128)S(1)} fusion(pred[8,33]{0,1:T(8,128)(4,1)S(1)} %copy-done.22, bf16[70,1,7,6,128]{4,2,3,0,1:T(8,128)(2,1)S(1)} %slice.85, bf16[70,1,8,33,128]{4,2,3,0,1:T(8,128)(2,1)S(1)} %copy.72, bf16[7,7,1,128]{3,1,0,2:T(8,128)(2,1)S(1)} %bitcast.146), kind=kOutput, calls=%fused_computation.69 | convolution fusion | flops 230879232 | bytes 14147080 | tf_op jit(solution)/shard_map/conv_general_dilated | solution.py:53
  567.7 4.9 copy.74
  572.6 6.2 %fusion.28 = f32[1,64,256,128]{3,1,2,0:T(8,128)S(1)} fusion(f32[64,1,264,128]{3,0,2,1:T(8,128)} %bitcast.133, bf16[1,64,256,128]{3,2,1,0:T(8,128)(2,1)S(1)} %copy-done.5), kind=kLoop, calls=%fused_computation.50 | loop fusion | flops 4194304 | bytes 20971520 | tf_op jit(solution)/shard_map/add | solution.py:165
  582.2 7.6 %scatter-add.4 = f32[1,64,256,128]{3,1,2,0:T(8,128)} dynamic-update-slice(f32[1,64,256,128]{3,1,2,0:T(8,128)} %copy-done.4, f32[1,3,256,128]{3,1,2,0:T(4,128)S(1)} %fusion.51, s32[]{:T(128)} %constant.89.clone.1, s32[]{:T(128)} %constant.94.clone.1, s32[]{:T(128)} %constant.89.clone.1, s32[]{:T(128)} %constant.89.clone.1) | dynamic-update-slice | bytes 786436 | tf_op jit(solution)/shard_map/scatter-add | solution.py:166
  589.8 4.5 convert_element_type.43
  594.3 4.7 copy.82
  (196 shorter events, 143.6 us)
Async XLA Ops:
  7.2 501.1 %all-reduce.4.cloned.1.call-start = ((), (), s32[]{:S(2)}) async-start(), calls=%async_computation | async-start | bytes 524288 | tf_op jit(solution)/shard_map/psum | solution.py:175
  19.1 12.2 %collective-permute-start.1 = (bf16[1,3,256,128]{3,0,2,1:T(2,128)(2,1)S(1)}, bf16[1,3,256,128]{3,0,2,1:T(2,128)(2,1)S(1)}, u32[]{:S(2)}, u32[]{:S(2)}) collective-permute-start(bf16[1,3,256,128]{3,0,2,1:T(2,128)(2,1)S(1)} %get-tuple-element.224), channel_id=1, source_target_pairs={{0,4},{4,0},{8,12},{12,8},{1,5},{5,1},{9,13},{13,9},{2,6},{6,2},{1... | collective-permute-start | bytes 589832 | tf_op jit(solution)/shard_map/ppermute | solution.py:35
  22.1 15.3 %collective-permute-start.3 = (bf16[1,3,256,128]{3,0,2,1:T(2,128)(2,1)S(1)}, bf16[1,3,256,128]{3,0,2,1:T(2,128)(2,1)S(1)}, u32[]{:S(2)}, u32[]{:S(2)}) collective-permute-start(bf16[1,3,256,128]{3,0,2,1:T(2,128)(2,1)S(1)} %get-tuple-element.225), channel_id=1, source_target_pairs={{2,0},{3,1},{6,4},{7,5},{10,8},{11,9},{14,12},{15,13},{18,16},{19,... | collective-permute-start | bytes 589832 | tf_op jit(solution)/shard_map/ppermute | solution.py:23
  31.3 19.6 %collective-permute-start.2 = (bf16[1,3,256,128]{3,0,2,1:T(2,128)(2,1)S(1)}, bf16[1,3,256,128]{3,0,2,1:T(2,128)(2,1)S(1)}, u32[]{:S(2)}, u32[]{:S(2)}) collective-permute-start(bf16[1,3,256,128]{3,0,2,1:T(2,128)(2,1)S(1)} %collective-permute-done.1), channel_id=1, source_target_pairs={{0,8},{8,0},{4,12},{12,4},{1,9},{9,1},{5,13},{13,5},{2,10},{10,2},... | collective-permute-start | bytes 589832 | tf_op jit(solution)/shard_map/ppermute | solution.py:35
  34.0 17.5 %collective-permute-start = (bf16[1,3,256,128]{3,0,2,1:T(2,128)(2,1)S(1)}, bf16[1,3,256,128]{3,0,2,1:T(2,128)(2,1)S(1)}, u32[]{:S(2)}, u32[]{:S(2)}) collective-permute-start(bf16[1,3,256,128]{3,0,2,1:T(2,128)(2,1)S(1)} %get-tuple-element.224), channel_id=1, source_target_pairs={{0,2},{1,3},{4,6},{5,7},{8,10},{9,11},{12,14},{13,15},{16,18},{17,... | collective-permute-start | bytes 589832 | tf_op jit(solution)/shard_map/ppermute | solution.py:20
  52.8 10.1 %collective-permute-start.4 = (bf16[1,70,3,128]{3,0,2,1:T(2,128)(2,1)S(1)}, bf16[1,70,3,128]{3,0,2,1:T(2,128)(2,1)S(1)}, u32[]{:S(2)}, u32[]{:S(2)}) collective-permute-start(bf16[1,70,3,128]{3,0,2,1:T(2,128)(2,1)S(1)} %get-tuple-element.222), channel_id=1, source_target_pairs={{0,4},{4,8},{8,12},{12,0},{1,5},{5,9},{9,13},{13,1},{2,6},{6,10},{... | collective-permute-start | bytes 161288 | tf_op jit(solution)/shard_map/ppermute | solution.py:20
  53.4 9.5 %collective-permute-start.5 = (bf16[1,70,3,128]{3,0,2,1:T(2,128)(2,1)S(1)}, bf16[1,70,3,128]{3,0,2,1:T(2,128)(2,1)S(1)}, u32[]{:S(2)}, u32[]{:S(2)}) collective-permute-start(bf16[1,70,3,128]{3,0,2,1:T(2,128)(2,1)S(1)} %get-tuple-element.223), channel_id=1, source_target_pairs={{4,0},{8,4},{12,8},{0,12},{5,1},{9,5},{13,9},{1,13},{6,2},{10,6},{... | collective-permute-start | bytes 161288 | tf_op jit(solution)/shard_map/ppermute | solution.py:23
  160.5 6.6 %copy-start.8 = (bf16[4,4096,128]{2,1,0:T(8,128)(2,1)S(1)}, bf16[4,4096,128]{2,1,0:T(8,128)(2,1)}, u32[]{:S(2)}) copy-start(bf16[4,4096,128]{2,1,0:T(8,128)(2,1)} %get-tuple-element.391) | copy-start | bytes 12582916 | tf_op jit(solution)/shard_map/while
  167.1 6.6 %slice-start = ((s8[8388608]{0:T(1024)(128)(4,1)}), s8[4194304]{0:T(1024)(128)(4,1)S(1)}, s32[]{:S(2)}) async-start(s8[8388608]{0:T(1024)(128)(4,1)} %bitcast.125), calls=%async_computation.1 | async-start | bytes 8388608 | tf_op jit(solution)/shard_map/while
  185.0 6.6 %copy-start.8 = (bf16[4,4096,128]{2,1,0:T(8,128)(2,1)S(1)}, bf16[4,4096,128]{2,1,0:T(8,128)(2,1)}, u32[]{:S(2)}) copy-start(bf16[4,4096,128]{2,1,0:T(8,128)(2,1)} %get-tuple-element.391) | copy-start | bytes 12582916 | tf_op jit(solution)/shard_map/while
  191.6 6.6 %slice-start = ((s8[8388608]{0:T(1024)(128)(4,1)}), s8[4194304]{0:T(1024)(128)(4,1)S(1)}, s32[]{:S(2)}) async-start(s8[8388608]{0:T(1024)(128)(4,1)} %bitcast.125), calls=%async_computation.1 | async-start | bytes 8388608 | tf_op jit(solution)/shard_map/while
  209.5 6.6 %copy-start.8 = (bf16[4,4096,128]{2,1,0:T(8,128)(2,1)S(1)}, bf16[4,4096,128]{2,1,0:T(8,128)(2,1)}, u32[]{:S(2)}) copy-start(bf16[4,4096,128]{2,1,0:T(8,128)(2,1)} %get-tuple-element.391) | copy-start | bytes 12582916 | tf_op jit(solution)/shard_map/while
  216.2 6.6 %slice-start = ((s8[8388608]{0:T(1024)(128)(4,1)}), s8[4194304]{0:T(1024)(128)(4,1)S(1)}, s32[]{:S(2)}) async-start(s8[8388608]{0:T(1024)(128)(4,1)} %bitcast.125), calls=%async_computation.1 | async-start | bytes 8388608 | tf_op jit(solution)/shard_map/while
  234.1 6.6 %copy-start.8 = (bf16[4,4096,128]{2,1,0:T(8,128)(2,1)S(1)}, bf16[4,4096,128]{2,1,0:T(8,128)(2,1)}, u32[]{:S(2)}) copy-start(bf16[4,4096,128]{2,1,0:T(8,128)(2,1)} %get-tuple-element.391) | copy-start | bytes 12582916 | tf_op jit(solution)/shard_map/while
  240.7 6.6 %slice-start = ((s8[8388608]{0:T(1024)(128)(4,1)}), s8[4194304]{0:T(1024)(128)(4,1)S(1)}, s32[]{:S(2)}) async-start(s8[8388608]{0:T(1024)(128)(4,1)} %bitcast.125), calls=%async_computation.1 | async-start | bytes 8388608 | tf_op jit(solution)/shard_map/while
  261.7 94.0 %copy-start.1 = (bf16[1,64,4,64,128]{4,3,2,1,0:T(8,128)(2,1)}, bf16[1,64,4,64,128]{4,3,2,1,0:T(8,128)(2,1)S(1)}, u32[]{:S(2)}) copy-start(bf16[1,64,4,64,128]{4,3,2,1,0:T(8,128)(2,1)S(1)} %copy.65) | copy-start | bytes 12582916
  262.1 154.7 %collective-permute-start.7 = (bf16[1,3,256,128]{3,0,2,1:T(2,128)(2,1)S(1)}, bf16[1,3,256,128]{3,0,2,1:T(2,128)(2,1)S(1)}, u32[]{:S(2)}, u32[]{:S(2)}) collective-permute-start(bf16[1,3,256,128]{3,0,2,1:T(2,128)(2,1)S(1)} %copy.87), channel_id=1, source_target_pairs={{0,4},{4,0},{8,12},{12,8},{1,5},{5,1},{9,13},{13,9},{2,6},{6,2},{1... | collective-permute-start | bytes 589832 | tf_op jit(solution)/shard_map/ppermute | solution.py:35
  262.1 247.8 %collective-permute-start.6 = (bf16[1,3,256,128]{3,0,2,1:T(2,128)(2,1)S(1)}, bf16[1,3,256,128]{3,0,2,1:T(2,128)(2,1)S(1)}, u32[]{:S(2)}, u32[]{:S(2)}) collective-permute-start(bf16[1,3,256,128]{3,0,2,1:T(2,128)(2,1)S(1)} %copy.87), channel_id=1, source_target_pairs={{0,2},{1,3},{4,6},{5,7},{8,10},{9,11},{12,14},{13,15},{16,18},{17,... | collective-permute-start | bytes 589832 | tf_op jit(solution)/shard_map/ppermute | solution.py:20
  414.9 95.1 %collective-permute-start.9 = (bf16[1,3,256,128]{3,0,2,1:T(2,128)(2,1)S(1)}, bf16[1,3,256,128]{3,0,2,1:T(2,128)(2,1)S(1)}, u32[]{:S(2)}, u32[]{:S(2)}) collective-permute-start(bf16[1,3,256,128]{3,0,2,1:T(2,128)(2,1)S(1)} %copy.88), channel_id=1, source_target_pairs={{2,0},{3,1},{6,4},{7,5},{10,8},{11,9},{14,12},{15,13},{18,16},{19,... | collective-permute-start | bytes 589832 | tf_op jit(solution)/shard_map/ppermute | solution.py:23
  416.7 93.2 %collective-permute-start.8 = (bf16[1,3,256,128]{3,0,2,1:T(2,128)(2,1)S(1)}, bf16[1,3,256,128]{3,0,2,1:T(2,128)(2,1)S(1)}, u32[]{:S(2)}, u32[]{:S(2)}) collective-permute-start(bf16[1,3,256,128]{3,0,2,1:T(2,128)(2,1)S(1)} %collective-permute-done.7), channel_id=1, source_target_pairs={{0,8},{8,0},{4,12},{12,4},{1,9},{9,1},{5,13},{13,5},{2,10},{10,2},... | collective-permute-start | bytes 589832 | tf_op jit(solution)/shard_map/ppermute | solution.py:35
  508.3 7.3 %copy-start.13 = (f32[256,128]{1,0:T(8,128)S(1)}, f32[256,128]{1,0:T(8,128)}, u32[]{:S(2)}) copy-start(f32[256,128]{1,0:T(8,128)} %get-tuple-element.212) | copy-start | bytes 393220
  508.3 10.9 %copy-start.2 = (bf16[1,64,4,64,128]{4,3,2,1,0:T(8,128)(2,1)S(1)}, bf16[1,64,4,64,128]{4,3,2,1,0:T(8,128)(2,1)}, u32[]{:S(2)}) copy-start(bf16[1,64,4,64,128]{4,3,2,1,0:T(8,128)(2,1)} %copy-done.1) | copy-start | bytes 12582916
  511.7 6.9 %collective-permute-start.10 = (bf16[1,70,3,128]{3,2,1,0:T(4,128)(2,1)S(1)}, bf16[1,70,3,128]{3,2,1,0:T(4,128)(2,1)S(1)}, u32[]{:S(2)}, u32[]{:S(2)}) collective-permute-start(bf16[1,70,3,128]{3,2,1,0:T(4,128)(2,1)S(1)} %get-tuple-element.226), channel_id=1, source_target_pairs={{0,4},{4,8},{8,12},{12,0},{1,5},{5,9},{9,13},{13,1},{2,6},{6,10},{... | collective-permute-start | bytes 161288 | tf_op jit(solution)/shard_map/ppermute | solution.py:20
  514.7 4.5 collective-permute-start.11
  (23 other events, 83.0 us)
Sparse Core Ops, SparseCore 0:
  416.3 91.9 all-reduce.3
where the time goes:
time: 611 us; the launch traced here: 606 us
  matrix products  218 us (36%)
  waiting for transfers between devices  115 us (19%)
  other arithmetic  110 us (18%)
  local copies, waits for them, and re-layouts  66.8 us (11%)
  blocking collectives  57.7 us (9%)
  starting transfers between devices  23 us (4%)
  between operations  14.9 us (2%)
    psum x1, waiting for transfers between devices, local(): lax.psum((g_in, g_out, g_kernel, g_bias, g_gain, g_shift, g_bin), ('lon',...  91 us
    conv_general_dilated x1, matrix products, kernel_grad(): lax.conv_general_dilated(extended[None], delta[:, :, None, :], (1, 1), 'V...  90.3 us
    conv_general_dilated x3, matrix products, conv_valid(): lax.conv_general_dilated(extended, kernel[:, :, None, :], (1, 1), 'VALID'...  68.3 us
    psum x1, blocking collectives, local(): lax.psum((g_in, g_out, g_kernel, g_bias, g_gain, g_shift, g_bin), ('lon',...  57.7 us
    concatenate x2, other arithmetic, padded(): block = jnp.concatenate([low, block, high], axis=dim)  47.6 us
    unnamed x52, local copies, waits for them, and re-layouts  25.1 us
    ppermute x4, waiting for transfers between devices, partner(): return lax.ppermute(block, axis, route)  21.3 us
    dynamic_update_slice x4, other arithmetic, local(): lax.scan(step, totals, (to_blocks(field_y), to_blocks(cotangent), masks))  16.5 us
  transfers between devices with their start and end apart: 13, of which 5 were waited for; matrix products, arithmetic and copies ran while one was open for 17% of the time, Pallas kernels for 0%

commit v1 on v0

--- a/solution.py
+++ b/solution.py
@@ -172,7 +172,9 @@
     scale = 1.0 / math.sqrt(cells_all)
     in_share = chans // lax.axis_size("dp")
     out_share = hidden // lax.axis_size("dp")
-    summed = lax.psum((g_in, g_out, g_kernel, g_bias, g_gain, g_shift, g_bin), ("lon", "lat", "dp"))
+    summed = lax.psum(
+        lax.psum((g_in, g_out, g_kernel, g_bias, g_gain, g_shift, g_bin), ("lat", "dp")), "lon"
+    )
     s_in, s_out, s_kernel, s_bias, s_gain, s_shift, s_bin = summed
     position = lax.axis_index("dp")
     s_in = lax.dynamic_slice_in_dim(s_in, position * in_share, in_share, 0)

time: 611 us -> 554 us (0.907)
  waiting for transfers between devices: 115 us -> 83.7 us
  blocking collectives: 57.7 us -> 28 us
    psum x1 -> x2, blocking collectives: 57.7 us -> 28 us  [the longest x1 17.7 us: local(): lax.psum(lax.psum((g_in, g_out, g_kernel, g_bias, g_gain, g_shift, g_bin)...]
    psum x1 -> x2, waiting for transfers between devices: 91 us -> 62.4 us  [the longest x1 32.4 us: local(): lax.psum(lax.psum((g_in, g_out, g_kernel, g_bias, g_gain, g_shift, g_bin)...]
    unnamed x52 -> x50, local copies, waits for them, and re-layouts: 25.1 us -> 26.3 us
  transfers between devices with their start and end apart: 13 -> 14, of which waited for: 5 -> 4; matrix products, arithmetic and copies ran while one was open for 17% -> 19% of each run, Pallas kernels for 0% -> 0%
where the time goes in v1:
time: 554 us; the launch traced here: 549 us
  matrix products  218 us (39%)
  other arithmetic  112 us (20%)
  waiting for transfers between devices  83.7 us (15%)
  local copies, waits for them, and re-layouts  68.2 us (12%)
  blocking collectives  28 us (5%)
  starting transfers between devices  23.6 us (4%)
  between operations  14.9 us (3%)
    conv_general_dilated x1, matrix products, kernel_grad(): lax.conv_general_dilated(extended[None], delta[:, :, None, :], (1, 1), 'V...  90.3 us
    conv_general_dilated x3, matrix products, conv_valid(): lax.conv_general_dilated(extended, kernel[:, :, None, :], (1, 1), 'VALID'...  68.3 us
    concatenate x2, other arithmetic, padded(): block = jnp.concatenate([low, block, high], axis=dim)  49.1 us
    psum x1, waiting for transfers between devices, local(): lax.psum(lax.psum((g_in, g_out, g_kernel, g_bias, g_gain, g_shift, g_bin)...  32.4 us
    psum x1, waiting for transfers between devices, local(): lax.psum((g_in, g_out, g_kernel, g_bias, g_gain, g_shift, g_bin), ('lat',...  30 us
    unnamed x50, local copies, waits for them, and re-layouts  26.3 us
    ppermute x4, waiting for transfers between devices, partner(): return lax.ppermute(block, axis, route)  21.3 us
    psum x1, blocking collectives, local(): lax.psum(lax.psum((g_in, g_out, g_kernel, g_bias, g_gain, g_shift, g_bin)...  17.7 us
  transfers between devices with their start and end apart: 14, of which 4 were waited for; matrix products, arithmetic and copies ran while one was open for 19% of the time, Pallas kernels for 0%

profile of v1, /device:TPU:0, one launch (start us, length us, event | category | flops | bytes accessed | tf_op | source)
XLA Modules:
  0.0 549.2 jit_solution(4856750972362839399)
XLA Ops:
  7.2 7.8 %copy.54 = bf16[1,64,256,128]{3,0,2,1:T(2,128)(2,1)S(1)} copy(bf16[1,64,256,128]{3,2,1,0:T(8,128)(2,1)} %param.14) | data formatting | bytes 8388608 | tf_op args[0]
  23.4 7.8 %collective-permute-done.1 = bf16[1,3,256,128]{3,0,2,1:T(2,128)(2,1)S(1)} collective-permute-done((bf16[1,3,256,128]{3,0,2,1:T(2,128)(2,1)S(1)}, bf16[1,3,256,128]{3,0,2,1:T(2,128)(2,1)S(1)}, u32[]{:S(2)}, u32[]{:S(2)}) %collective-permute-start.1) | collective-permute-done | bytes 196640 | tf_op jit(solution)/shard_map/ppermute | solution.py:35
  37.4 13.4 %collective-permute-done.2 = bf16[1,3,256,128]{3,0,2,1:T(2,128)(2,1)S(1)} collective-permute-done((bf16[1,3,256,128]{3,0,2,1:T(2,128)(2,1)S(1)}, bf16[1,3,256,128]{3,0,2,1:T(2,128)(2,1)S(1)}, u32[]{:S(2)}, u32[]{:S(2)}) %collective-permute-start.2) | collective-permute-done | bytes 196640 | tf_op jit(solution)/shard_map/ppermute | solution.py:35
  57.4 5.5 %copy.64 = bf16[1,64,4,64,128]{4,3,1,2,0:T(8,128)(2,1)} copy(bf16[1,64,4,64,128]{4,3,2,1,0:T(8,128)(2,1)} %bitcast.138) | data formatting | bytes 8388608 | tf_op jit(solution)/shard_map/reshape | solution.py:124
  62.9 41.8 %pad_maximum_fusion = bf16[1,70,262,128]{3,0,2,1:T(2,128)(2,1)S(1)} fusion(bf16[1,70,3,128]{3,0,2,1:T(2,128)(2,1)S(1)} %collective-permute-done.5, bf16[1,3,256,128]{3,0,2,1:T(2,128)(2,1)S(1)} %broadcast_select_fusion.4, bf16[1,64,256,128]{3,0,2,1:T(2,128)(2,1)} %copy-done, bf16[1,3,256,128]{3,0,2,1:T(2,128)(2,1)S(1)} %collective-permute-done, ...), kind=kLoop, calls=%fused_computation.47 | loop fusion | flops 9390080 | bytes 9390080 | tf_op jit(solution)/shard_map/concatenate | solution.py:24
  110.8 34.0 %select_add_fusion.1 = f32[64,8,33,128]{3,1,2,0:T(8,128)S(1)} fusion(f32[128]{0:T(128)S(1)} %copy-done.19, pred[8,33]{0,1:T(8,128)(4,1)S(1)} %copy-done.20, bf16[70,1,7,6,128]{4,2,3,0,1:T(8,128)(2,1)S(1)} %slice.80, bf16[70,1,8,33,128]{4,2,3,0,1:T(8,128)(2,1)S(1)} %copy.59, bf16[7,7,1,128]{3,1,0,2:T(8,128)(2,1)S(1)} %bitcast.144), kind=kOutput, calls=%fused_computation.48 | convolution fusion | flops 233041920 | bytes 14147592 | tf_op jit(solution)/shard_map/conv_general_dilated | solution.py:53
  148.2 4.9 copy.62
  153.1 4.2 copy.63
  157.3 98.5 %while.22 = (s32[]{:T(128)}, f32[128,256]{1,0:T(8,128)S(1)}, f32[256]{0:T(256)S(1)}, f32[256,128]{1,0:T(8,128)S(1)}, f32[128]{0:T(128)S(1)}, /*index=5*/f32[128]...) while((s32[]{:T(128)}, f32[128,256]{1,0:T(8,128)S(1)}, ...), condition=%wide.region_8.9_spmd.clone, body=%wide.region_0.8_spmd.clone.sunk | while | flops 1393168896 | bytes 81850672 | solution.py:141
  178.1 4.1 fusion.106
  227.1 4.1 fusion.106
  255.7 4.5 convert_reduce_fusion
  265.4 90.3 %fusion.29 = f32[1,7,7,128]{3,0,2,1:T(1,128)S(1)} fusion(bf16[1,70,262,128]{3,0,2,1:T(2,128)(2,1)} %copy-done.3, bf16[64,256,1,128]{3,1,0,2:T(8,128)(2,1)S(1)} %bitcast.128), kind=kOutput, calls=%fused_computation.51 | convolution fusion | flops 205520896 | bytes 8914432 | tf_op jit(solution)/shard_map/conv_general_dilated | solution.py:65
  355.7 10.3 %all-reduce = (f32[7,7,128]{2,1,0:T(8,128)S(1)}, f32[128]{0:T(128)S(1)}, f32[128]{0:T(128)S(1)}, f32[128]{0:T(128)S(1)}, f32[256]{0:T(256)S(1)}) all-reduce(f32[7,7,128]{2,1,0:T(8,128)S(1)} %bitcast.143, f32[128]{0:T(128)S(1)} %convert_reduce_fusion, ...), channel_id=1, replica_groups=mesh['groups'=2,'lon'=4,'lat'=2,'dp'=2] {'lat','dp'}, use_global_device_ids=true, to_apply=%region_13.14 | all-reduce | flops 6912 | bytes 55296 | tf_op jit(solution)/shard_map/psum | solution.py:176
  366.0 17.7 %all-reduce.2 = (f32[7,7,128]{2,1,0:T(8,128)S(1)}, f32[128]{0:T(128)S(1)}, f32[128]{0:T(128)S(1)}, f32[128]{0:T(128)S(1)}, f32[256]{0:T(256)S(1)}) all-reduce(f32[7,7,128]{2,1,0:T(8,128)S(1)} %get-tuple-element.206, f32[128]{0:T(128)S(1)} %get-tuple-element.207, ...), channel_id=1, replica_groups=mesh['groups'=2,'lon'=4,'lat'=2,'dp'=2] {'lon'}, use_global_device_ids=true, to_apply=%region_14.15 | all-reduce | flops 6912 | bytes 55296 | tf_op jit(solution)/shard_map/psum | solution.py:175
  388.3 30.0 %all-reduce.7.cloned.1.call-done = (f32[128,256]{1,0:T(8,128)}, f32[256,128]{1,0:T(8,128)}) async-done(((f32[128,256]{1,0:T(8,128)}, f32[256,128]{1,0:T(8,128)}), (f32[128,256]{1,0:T(8,128)}, f32[256,128]{1,0:T(8,128)})) %all-reduce.7.cloned.1.call-update) | async-done | bytes 262160 | tf_op jit(solution)/shard_map/psum | solution.py:176
  423.9 32.4 %all-reduce.9.cloned.1.call-done = (f32[128,256]{1,0:T(8,128)}, f32[256,128]{1,0:T(8,128)}) async-done(((f32[128,256]{1,0:T(8,128)}, f32[256,128]{1,0:T(8,128)}), (f32[128,256]{1,0:T(8,128)}, f32[256,128]{1,0:T(8,128)})) %all-reduce.9.cloned.1.call-update) | async-done | bytes 262160 | tf_op jit(solution)/shard_map/psum | solution.py:175
  459.3 7.3 %pad_maximum_fusion.1 = bf16[1,70,262,128]{3,2,1,0:T(8,128)(2,1)S(1)} fusion(bf16[1,70,3,128]{3,2,1,0:T(4,128)(2,1)S(1)} %collective-permute-done.11, bf16[1,3,256,128]{3,2,1,0:T(8,128)(2,1)S(1)} %copy.69, bf16[1,64,256,128]{3,2,1,0:T(8,128)(2,1)} %bitcast.130, bf16[1,3,256,128]{3,2,1,0:T(8,128)(2,1)S(1)} %copy.68, ...), kind=kLoop, calls=%fused_computation.66 | loop fusion | flops 23475200 | bytes 9390080 | tf_op jit(solution)/shard_map/concatenate | solution.py:24
  477.2 33.5 %broadcast_select_fusion.2 = f32[64,8,33,128]{3,1,2,0:T(8,128)S(1)} fusion(pred[8,33]{0,1:T(8,128)(4,1)S(1)} %copy-done.21, bf16[70,1,7,6,128]{4,2,3,0,1:T(8,128)(2,1)S(1)} %slice.85, bf16[70,1,8,33,128]{4,2,3,0,1:T(8,128)(2,1)S(1)} %copy.72, bf16[7,7,1,128]{3,1,0,2:T(8,128)(2,1)S(1)} %bitcast.146), kind=kOutput, calls=%fused_computation.69 | convolution fusion | flops 230879232 | bytes 14147080 | tf_op jit(solution)/shard_map/conv_general_dilated | solution.py:53
  510.7 4.9 copy.74
  515.7 6.2 %fusion.28 = f32[1,64,256,128]{3,1,2,0:T(8,128)S(1)} fusion(f32[64,1,264,128]{3,0,2,1:T(8,128)} %bitcast.133, bf16[1,64,256,128]{3,2,1,0:T(8,128)(2,1)S(1)} %copy-done.5), kind=kLoop, calls=%fused_computation.50 | loop fusion | flops 4194304 | bytes 20971520 | tf_op jit(solution)/shard_map/add | solution.py:165
  525.3 7.6 %scatter-add.4 = f32[1,64,256,128]{3,1,2,0:T(8,128)} dynamic-update-slice(f32[1,64,256,128]{3,1,2,0:T(8,128)} %copy-done.4, f32[1,3,256,128]{3,1,2,0:T(4,128)S(1)} %fusion.51, s32[]{:T(128)} %constant.89.clone.1, s32[]{:T(128)} %constant.94.clone.1, s32[]{:T(128)} %constant.89.clone.1, s32[]{:T(128)} %constant.89.clone.1) | dynamic-update-slice | bytes 786436 | tf_op jit(solution)/shard_map/scatter-add | solution.py:166
  532.9 4.5 convert_element_type.43
  537.4 4.7 copy.82
  (198 shorter events, 151.7 us)
Async XLA Ops:
  7.2 411.1 %all-reduce.7.cloned.1.call-start = ((), (), s32[]{:S(2)}) async-start(), calls=%async_computation | async-start | bytes 524288 | tf_op jit(solution)/shard_map/psum | solution.py:176
  19.0 12.2 %collective-permute-start.1 = (bf16[1,3,256,128]{3,0,2,1:T(2,128)(2,1)S(1)}, bf16[1,3,256,128]{3,0,2,1:T(2,128)(2,1)S(1)}, u32[]{:S(2)}, u32[]{:S(2)}) collective-permute-start(bf16[1,3,256,128]{3,0,2,1:T(2,128)(2,1)S(1)} %get-tuple-element.231), channel_id=1, source_target_pairs={{0,4},{4,0},{8,12},{12,8},{1,5},{5,1},{9,13},{13,9},{2,6},{6,2},{1... | collective-permute-start | bytes 589832 | tf_op jit(solution)/shard_map/ppermute | solution.py:35
  22.1 15.3 %collective-permute-start.3 = (bf16[1,3,256,128]{3,0,2,1:T(2,128)(2,1)S(1)}, bf16[1,3,256,128]{3,0,2,1:T(2,128)(2,1)S(1)}, u32[]{:S(2)}, u32[]{:S(2)}) collective-permute-start(bf16[1,3,256,128]{3,0,2,1:T(2,128)(2,1)S(1)} %get-tuple-element.232), channel_id=1, source_target_pairs={{2,0},{3,1},{6,4},{7,5},{10,8},{11,9},{14,12},{15,13},{18,16},{19,... | collective-permute-start | bytes 589832 | tf_op jit(solution)/shard_map/ppermute | solution.py:23
  31.3 19.6 %collective-permute-start.2 = (bf16[1,3,256,128]{3,0,2,1:T(2,128)(2,1)S(1)}, bf16[1,3,256,128]{3,0,2,1:T(2,128)(2,1)S(1)}, u32[]{:S(2)}, u32[]{:S(2)}) collective-permute-start(bf16[1,3,256,128]{3,0,2,1:T(2,128)(2,1)S(1)} %collective-permute-done.1), channel_id=1, source_target_pairs={{0,8},{8,0},{4,12},{12,4},{1,9},{9,1},{5,13},{13,5},{2,10},{10,2},... | collective-permute-start | bytes 589832 | tf_op jit(solution)/shard_map/ppermute | solution.py:35
  34.0 17.5 %collective-permute-start = (bf16[1,3,256,128]{3,0,2,1:T(2,128)(2,1)S(1)}, bf16[1,3,256,128]{3,0,2,1:T(2,128)(2,1)S(1)}, u32[]{:S(2)}, u32[]{:S(2)}) collective-permute-start(bf16[1,3,256,128]{3,0,2,1:T(2,128)(2,1)S(1)} %get-tuple-element.231), channel_id=1, source_target_pairs={{0,2},{1,3},{4,6},{5,7},{8,10},{9,11},{12,14},{13,15},{16,18},{17,... | collective-permute-start | bytes 589832 | tf_op jit(solution)/shard_map/ppermute | solution.py:20
  52.8 10.1 %collective-permute-start.4 = (bf16[1,70,3,128]{3,0,2,1:T(2,128)(2,1)S(1)}, bf16[1,70,3,128]{3,0,2,1:T(2,128)(2,1)S(1)}, u32[]{:S(2)}, u32[]{:S(2)}) collective-permute-start(bf16[1,70,3,128]{3,0,2,1:T(2,128)(2,1)S(1)} %get-tuple-element.229), channel_id=1, source_target_pairs={{0,4},{4,8},{8,12},{12,0},{1,5},{5,9},{9,13},{13,1},{2,6},{6,10},{... | collective-permute-start | bytes 161288 | tf_op jit(solution)/shard_map/ppermute | solution.py:20
  53.4 9.5 %collective-permute-start.5 = (bf16[1,70,3,128]{3,0,2,1:T(2,128)(2,1)S(1)}, bf16[1,70,3,128]{3,0,2,1:T(2,128)(2,1)S(1)}, u32[]{:S(2)}, u32[]{:S(2)}) collective-permute-start(bf16[1,70,3,128]{3,0,2,1:T(2,128)(2,1)S(1)} %get-tuple-element.230), channel_id=1, source_target_pairs={{4,0},{8,4},{12,8},{0,12},{5,1},{9,5},{13,9},{1,13},{6,2},{10,6},{... | collective-permute-start | bytes 161288 | tf_op jit(solution)/shard_map/ppermute | solution.py:23
  160.5 6.6 %copy-start.8 = (bf16[4,4096,128]{2,1,0:T(8,128)(2,1)S(1)}, bf16[4,4096,128]{2,1,0:T(8,128)(2,1)}, u32[]{:S(2)}) copy-start(bf16[4,4096,128]{2,1,0:T(8,128)(2,1)} %get-tuple-element.398) | copy-start | bytes 12582916 | tf_op jit(solution)/shard_map/while
  167.1 6.6 %slice-start = ((s8[8388608]{0:T(1024)(128)(4,1)}), s8[4194304]{0:T(1024)(128)(4,1)S(1)}, s32[]{:S(2)}) async-start(s8[8388608]{0:T(1024)(128)(4,1)} %bitcast.125), calls=%async_computation.2 | async-start | bytes 8388608 | tf_op jit(solution)/shard_map/while
  185.0 6.6 %copy-start.8 = (bf16[4,4096,128]{2,1,0:T(8,128)(2,1)S(1)}, bf16[4,4096,128]{2,1,0:T(8,128)(2,1)}, u32[]{:S(2)}) copy-start(bf16[4,4096,128]{2,1,0:T(8,128)(2,1)} %get-tuple-element.398) | copy-start | bytes 12582916 | tf_op jit(solution)/shard_map/while
  191.6 6.6 %slice-start = ((s8[8388608]{0:T(1024)(128)(4,1)}), s8[4194304]{0:T(1024)(128)(4,1)S(1)}, s32[]{:S(2)}) async-start(s8[8388608]{0:T(1024)(128)(4,1)} %bitcast.125), calls=%async_computation.2 | async-start | bytes 8388608 | tf_op jit(solution)/shard_map/while
  209.5 6.6 %copy-start.8 = (bf16[4,4096,128]{2,1,0:T(8,128)(2,1)S(1)}, bf16[4,4096,128]{2,1,0:T(8,128)(2,1)}, u32[]{:S(2)}) copy-start(bf16[4,4096,128]{2,1,0:T(8,128)(2,1)} %get-tuple-element.398) | copy-start | bytes 12582916 | tf_op jit(solution)/shard_map/while
  216.1 6.6 %slice-start = ((s8[8388608]{0:T(1024)(128)(4,1)}), s8[4194304]{0:T(1024)(128)(4,1)S(1)}, s32[]{:S(2)}) async-start(s8[8388608]{0:T(1024)(128)(4,1)} %bitcast.125), calls=%async_computation.2 | async-start | bytes 8388608 | tf_op jit(solution)/shard_map/while
  234.0 6.6 %copy-start.8 = (bf16[4,4096,128]{2,1,0:T(8,128)(2,1)S(1)}, bf16[4,4096,128]{2,1,0:T(8,128)(2,1)}, u32[]{:S(2)}) copy-start(bf16[4,4096,128]{2,1,0:T(8,128)(2,1)} %get-tuple-element.398) | copy-start | bytes 12582916 | tf_op jit(solution)/shard_map/while
  240.6 6.6 %slice-start = ((s8[8388608]{0:T(1024)(128)(4,1)}), s8[4194304]{0:T(1024)(128)(4,1)S(1)}, s32[]{:S(2)}) async-start(s8[8388608]{0:T(1024)(128)(4,1)} %bitcast.125), calls=%async_computation.2 | async-start | bytes 8388608 | tf_op jit(solution)/shard_map/while
  255.7 5.9 %copy-start.10 = (f32[256,128]{1,0:T(8,128)}, f32[256,128]{1,0:T(8,128)S(1)}, u32[]{:S(2)}) copy-start(f32[256,128]{1,0:T(8,128)S(1)} %get-tuple-element.104) | copy-start | bytes 393220
  261.7 94.0 %copy-start.1 = (bf16[1,64,4,64,128]{4,3,2,1,0:T(8,128)(2,1)}, bf16[1,64,4,64,128]{4,3,2,1,0:T(8,128)(2,1)S(1)}, u32[]{:S(2)}) copy-start(bf16[1,64,4,64,128]{4,3,2,1,0:T(8,128)(2,1)S(1)} %copy.65) | copy-start | bytes 12582916
  262.0 125.1 %collective-permute-start.7 = (bf16[1,3,256,128]{3,0,2,1:T(2,128)(2,1)S(1)}, bf16[1,3,256,128]{3,0,2,1:T(2,128)(2,1)S(1)}, u32[]{:S(2)}, u32[]{:S(2)}) collective-permute-start(bf16[1,3,256,128]{3,0,2,1:T(2,128)(2,1)S(1)} %copy.87), channel_id=1, source_target_pairs={{0,4},{4,0},{8,12},{12,8},{1,5},{5,1},{9,13},{13,9},{2,6},{6,2},{1... | collective-permute-start | bytes 589832 | tf_op jit(solution)/shard_map/ppermute | solution.py:35
  262.1 156.2 %collective-permute-start.6 = (bf16[1,3,256,128]{3,0,2,1:T(2,128)(2,1)S(1)}, bf16[1,3,256,128]{3,0,2,1:T(2,128)(2,1)S(1)}, u32[]{:S(2)}, u32[]{:S(2)}) collective-permute-start(bf16[1,3,256,128]{3,0,2,1:T(2,128)(2,1)S(1)} %copy.87), channel_id=1, source_target_pairs={{0,2},{1,3},{4,6},{5,7},{8,10},{9,11},{12,14},{13,15},{16,18},{17,... | collective-permute-start | bytes 589832 | tf_op jit(solution)/shard_map/ppermute | solution.py:20
  385.3 33.1 %collective-permute-start.9 = (bf16[1,3,256,128]{3,0,2,1:T(2,128)(2,1)S(1)}, bf16[1,3,256,128]{3,0,2,1:T(2,128)(2,1)S(1)}, u32[]{:S(2)}, u32[]{:S(2)}) collective-permute-start(bf16[1,3,256,128]{3,0,2,1:T(2,128)(2,1)S(1)} %copy.88), channel_id=1, source_target_pairs={{2,0},{3,1},{6,4},{7,5},{10,8},{11,9},{14,12},{15,13},{18,16},{19,... | collective-permute-start | bytes 589832 | tf_op jit(solution)/shard_map/ppermute | solution.py:23
  386.6 69.8 %all-reduce.9.cloned.1.call-start = ((), (), s32[]{:S(2)}) async-start(), calls=%async_computation.1 | async-start | bytes 524288 | tf_op jit(solution)/shard_map/psum | solution.py:175
  387.2 31.2 %collective-permute-start.8 = (bf16[1,3,256,128]{3,0,2,1:T(2,128)(2,1)S(1)}, bf16[1,3,256,128]{3,0,2,1:T(2,128)(2,1)S(1)}, u32[]{:S(2)}, u32[]{:S(2)}) collective-permute-start(bf16[1,3,256,128]{3,0,2,1:T(2,128)(2,1)S(1)} %collective-permute-done.7), channel_id=1, source_target_pairs={{0,8},{8,0},{4,12},{12,4},{1,9},{9,1},{5,13},{13,5},{2,10},{10,2},... | collective-permute-start | bytes 589832 | tf_op jit(solution)/shard_map/ppermute | solution.py:35
  420.0 39.3 %collective-permute-start.10 = (bf16[1,70,3,128]{3,2,1,0:T(4,128)(2,1)S(1)}, bf16[1,70,3,128]{3,2,1,0:T(4,128)(2,1)S(1)}, u32[]{:S(2)}, u32[]{:S(2)}) collective-permute-start(bf16[1,70,3,128]{3,2,1,0:T(4,128)(2,1)S(1)} %get-tuple-element.233), channel_id=1, source_target_pairs={{0,4},{4,8},{8,12},{12,0},{1,5},{5,9},{9,13},{13,1},{2,6},{6,10},{... | collective-permute-start | bytes 161288 | tf_op jit(solution)/shard_map/ppermute | solution.py:20
  421.6 37.7 %collective-permute-start.11 = (bf16[1,70,3,128]{3,2,1,0:T(4,128)(2,1)S(1)}, bf16[1,70,3,128]{3,2,1,0:T(4,128)(2,1)S(1)}, u32[]{:S(2)}, u32[]{:S(2)}) collective-permute-start(bf16[1,70,3,128]{3,2,1,0:T(4,128)(2,1)S(1)} %get-tuple-element.234), channel_id=1, source_target_pairs={{4,0},{8,4},{12,8},{0,12},{5,1},{9,5},{13,9},{1,13},{6,2},{10,6},{... | collective-permute-start | bytes 161288 | tf_op jit(solution)/shard_map/ppermute | solution.py:23
  (23 other events, 80.9 us)
Sparse Core Ops, SparseCore 0:
  386.7 31.4 all-reduce.6
  420.7 35.5 all-reduce.8
